TPU v7x, 32 devices: a whole 2x2x4 slice. The times are simulated.
32 devices in a mesh: dp: 8 (over z, x), ctx: 4 (over y, core).
Axes of the slice: x: 2, y: 2, z: 4, core: 2. Of those that a mesh axis runs over, the one named last changes fastest.
Arguments:
- layer_input: bfloat16 [16, 1024, 2048], P('dp', 'ctx'), may hold values from -6 to 6
- lengths: int32 [16], P('dp'), may hold values from 256 to 1024, as said below
- attn_gain: float32 [2048], replicated, may hold values from 0.5 to 1.5
- w_query: bfloat16 [2048, 1280], P('dp', 'ctx'), may hold values from -0.125 to 0.125
- w_key: bfloat16 [2048, 320], P('dp', 'ctx'), may hold values from -0.125 to 0.125
- w_value: bfloat16 [2048, 320], P('dp', 'ctx'), may hold values from -0.125 to 0.125
- query_gain: float32 [64], replicated, may hold values from 0.1 to 1.9
- key_gain: float32 [64], replicated, may hold values from 0.1 to 1.9
- w_out: bfloat16 [2048, 1280], P('dp', 'ctx'), may hold values from -3 to 3
- ffn_gain: float32 [2048], replicated, may hold values from 0.5 to 1.5
- w_gate: bfloat16 [2048, 5120], P('dp', 'ctx'), may hold values from -0.125 to 0.125
- w_up: bfloat16 [2048, 5120], P('dp', 'ctx'), may hold values from -0.125 to 0.125
- w_down: bfloat16 [2048, 5120], P('dp', 'ctx'), may hold values from -0.078125 to 0.078125
- cotangent: bfloat16 [16, 1024, 2048], P('dp', 'ctx'), may hold values from -6 to 6
Outputs:
- layer_output: bfloat16 [16, 1024, 2048], P('dp', 'ctx')
- input_grad: bfloat16 [16, 1024, 2048], P('dp', 'ctx')
- attn_gain_grad: float32 [2048], replicated
- w_query_grad: float32 [2048, 1280], P('dp', 'ctx')
- w_key_grad: float32 [2048, 320], P('dp', 'ctx')
- w_value_grad: float32 [2048, 320], P('dp', 'ctx')
- query_gain_grad: float32 [64], replicated
- key_gain_grad: float32 [64], replicated
- w_out_grad: float32 [2048, 1280], P('dp', 'ctx')
- ffn_gain_grad: float32 [2048], replicated
- w_gate_grad: float32 [2048, 5120], P('dp', 'ctx')
- w_up_grad: float32 [2048, 5120], P('dp', 'ctx')
- w_down_grad: float32 [2048, 5120], P('dp', 'ctx')
Inputs may be any that keep to these rules, and one draw needn't show every extreme that they name: `lengths`: some row has all 1024 slots valid.
All inputs are finite; a program needn't handle non-finite values.
Results may differ from a plain program's by a relative error of at most 0.02.
Values may be sent and summed in bfloat16 or wider, within the bound.
A program may use at most 384 MiB of HBM per device.

v0:
```python
import math
import jax
import jax.numpy as jnp
from jax import lax
from jax.sharding import PartitionSpec as P

D = 2048
HQ = 20
KVH = 5
HD = 64
SLOTS = 1024
EPSILON = 1e-06
ROPE_BASE = 10000.0


def norm_rows(values, gain_vec):
    scale_inv = lax.rsqrt(jnp.mean(values * values, -1, keepdims=True) + EPSILON)
    unit_rows = values * scale_inv
    return (unit_rows * gain_vec, unit_rows, scale_inv)


def norm_back(grad_unit, unit_rows, scale_inv):
    return scale_inv * (grad_unit - unit_rows * jnp.mean(grad_unit * unit_rows, -1, keepdims=True))


def rope_tables(positions, head_size):
    steps_half = jnp.arange(head_size // 2, dtype=jnp.float32)
    inverse = jnp.exp(steps_half * (-2.0 * math.log(ROPE_BASE) / head_size))
    angles = positions.astype(jnp.float32)[:, None] * inverse[None, :]
    cosine_table = jnp.concatenate([jnp.cos(angles), jnp.cos(angles)], -1)[:, None, :]
    sine_table = jnp.concatenate([jnp.sin(angles), jnp.sin(angles)], -1)[:, None, :]
    return (cosine_table, sine_table)


def rotate(values, cosine_table, sine_table):
    half_size = values.shape[-1] // 2
    turned = jnp.concatenate([-values[..., half_size:], values[..., :half_size]], -1)
    return values * cosine_table + turned * sine_table


def rotate_back(incoming, cosine_table, sine_table):
    half_size = incoming.shape[-1] // 2
    turned = incoming * sine_table
    return incoming * cosine_table + jnp.concatenate(
        [turned[..., half_size:], -turned[..., :half_size]], -1
    )


def contract_last(left_side, right_side):
    return lax.dot_general(
        left_side, right_side, (((1,), (1,)), ((), ())), preferred_element_type=jnp.float32
    )


def contract_rows(left_side, right_side):
    return lax.dot_general(
        left_side, right_side, (((0,), (0,)), ((), ())), preferred_element_type=jnp.float32
    )


def masked_scores(grouped, kv_block, allowed, kv_width, scaling):
    key_rows = kv_block[:, :kv_width].reshape(kv_block.shape[0], KVH, HD)
    raw_scores = (
        jnp.einsum("skgh,tkh->kgst", grouped, key_rows, preferred_element_type=jnp.float32)
        * scaling
    )
    return jnp.where(allowed, raw_scores, -1e30)


def per_device(
    layer_input,
    lengths,
    attn_gain,
    w_query,
    w_key,
    w_value,
    query_gain,
    key_gain,
    w_out,
    ffn_gain,
    w_gate,
    w_up,
    w_down,
    cotangent,
):
    micro_count = layer_input.shape[0]
    seq_len = layer_input.shape[1]
    group_size = HQ // KVH
    kv_width = KVH * HD
    q_width = HQ * HD
    scaling = 1.0 / math.sqrt(HD)
    positions = lax.axis_index("ctx") * seq_len + jnp.arange(seq_len, dtype=jnp.int32)
    key_slots = jnp.arange(SLOTS, dtype=jnp.int32)
    cosine_table, sine_table = rope_tables(positions, HD)
    causal = key_slots[None, :] <= positions[:, None]
    grad_attn_gain = jnp.zeros((D,), jnp.float32)
    grad_ffn_gain = jnp.zeros((D,), jnp.float32)
    grad_query_gain = jnp.zeros((HD,), jnp.float32)
    grad_key_gain = jnp.zeros((HD,), jnp.float32)
    stored = {
        "normed": [],
        "query": [],
        "key": [],
        "value": [],
        "mixed": [],
        "attn": [],
        "normed_two": [],
        "gate": [],
        "upper": [],
        "hidden": [],
        "branch": [],
    }
    out_rows = []
    input_grads = []
    columns = (
        lax.all_gather(w_query, "ctx", axis=1, tiled=True),
        lax.all_gather(w_key, "ctx", axis=1, tiled=True),
        lax.all_gather(w_value, "ctx", axis=1, tiled=True),
        lax.all_gather(w_out, "ctx", axis=1, tiled=True),
        lax.all_gather(w_gate, "ctx", axis=1, tiled=True),
        lax.all_gather(w_up, "ctx", axis=1, tiled=True),
        lax.all_gather(w_down, "ctx", axis=1, tiled=True),
    )
    gathered = (
        lax.all_gather(columns[0], "dp", axis=0, tiled=True),
        lax.all_gather(columns[1], "dp", axis=0, tiled=True),
        lax.all_gather(columns[2], "dp", axis=0, tiled=True),
        lax.all_gather(columns[3], "dp", axis=0, tiled=True),
        lax.all_gather(columns[4], "dp", axis=0, tiled=True),
        lax.all_gather(columns[5], "dp", axis=0, tiled=True),
        lax.all_gather(columns[6], "dp", axis=0, tiled=True),
    )
    for batch_index in range(micro_count):
        row_length = lengths[batch_index]
        mat_query, mat_key, mat_value, mat_out, mat_gate, mat_up, mat_down = gathered
        valid_mask = (positions < row_length).astype(jnp.float32)[:, None]
        allowed = causal & (key_slots < row_length)[None, :]
        row_input = layer_input[batch_index].astype(jnp.float32)
        normed_one, unit_one, inv_one = norm_rows(row_input, attn_gain)
        normed_bf = normed_one.astype(jnp.bfloat16)
        query_lin = jnp.dot(normed_bf, mat_query, preferred_element_type=jnp.float32)
        key_lin = jnp.dot(normed_bf, mat_key, preferred_element_type=jnp.float32)
        value_lin = jnp.dot(normed_bf, mat_value, preferred_element_type=jnp.float32)
        query_norm, query_unit, query_inv = norm_rows(
            query_lin.reshape(seq_len, HQ, HD), query_gain
        )
        key_norm, key_unit, key_inv = norm_rows(key_lin.reshape(seq_len, KVH, HD), key_gain)
        query_bf = rotate(query_norm, cosine_table, sine_table).astype(jnp.bfloat16)
        grouped = query_bf.reshape(seq_len, KVH, group_size, HD)
        key_bf = rotate(key_norm, cosine_table, sine_table).astype(jnp.bfloat16)
        value_bf = value_lin.astype(jnp.bfloat16)
        kv_local = jnp.concatenate([key_bf.reshape(seq_len, kv_width), value_bf], -1)
        kv_whole = lax.all_gather(kv_local, "ctx", axis=0, tiled=True)
        scores = masked_scores(grouped, kv_whole, allowed, kv_width, scaling)
        largest = jnp.max(scores, -1, keepdims=True)
        log_total = largest + jnp.log(jnp.sum(jnp.exp(scores - largest), -1, keepdims=True))
        probs_bf = jnp.exp(scores - log_total).astype(jnp.bfloat16)
        values_all = kv_whole[:, kv_width:].reshape(SLOTS, KVH, HD)
        mixed_bf = (
            jnp.einsum("kgst,tkh->skgh", probs_bf, values_all, preferred_element_type=jnp.float32)
            .reshape(seq_len, q_width)
            .astype(jnp.bfloat16)
        )
        middle = row_input + contract_last(mixed_bf, mat_out)
        normed_two, unit_two, inv_two = norm_rows(middle, ffn_gain)
        normed_two_bf = normed_two.astype(jnp.bfloat16)
        gate_lin = jnp.dot(normed_two_bf, mat_gate, preferred_element_type=jnp.float32)
        up_lin = jnp.dot(normed_two_bf, mat_up, preferred_element_type=jnp.float32)
        sigmoid_gate = jax.nn.sigmoid(gate_lin)
        activated = gate_lin * sigmoid_gate
        hidden_bf = (activated * up_lin).astype(jnp.bfloat16)
        branch = contract_last(hidden_bf, mat_down)
        out_rows.append((valid_mask * (middle + branch)).astype(jnp.bfloat16))
        mat_query, mat_key, mat_value, mat_out, mat_gate, mat_up, mat_down = gathered
        row_grad = cotangent[batch_index].astype(jnp.float32) * valid_mask
        branch_grad = row_grad.astype(jnp.bfloat16)
        hidden_grad = jnp.dot(branch_grad, mat_down, preferred_element_type=jnp.float32)
        gate_grad = (
            hidden_grad * up_lin * sigmoid_gate * (1.0 + gate_lin * (1.0 - sigmoid_gate))
        ).astype(jnp.bfloat16)
        up_grad = (hidden_grad * activated).astype(jnp.bfloat16)
        normed_two_grad = contract_last(gate_grad, mat_gate) + contract_last(up_grad, mat_up)
        grad_ffn_gain = grad_ffn_gain + jnp.sum(normed_two_grad * unit_two, 0)
        middle_grad = row_grad + norm_back(normed_two_grad * ffn_gain, unit_two, inv_two)
        attn_grad = middle_grad.astype(jnp.bfloat16)
        mixed_grad = (
            jnp.dot(attn_grad, mat_out, preferred_element_type=jnp.float32)
            .astype(jnp.bfloat16)
            .reshape(seq_len, KVH, group_size, HD)
        )
        kv_back = lax.all_gather(kv_local, "ctx", axis=0, tiled=True)
        scores = masked_scores(grouped, kv_back, allowed, kv_width, scaling)
        probs = jnp.exp(scores - log_total)
        keys_back = kv_back[:, :kv_width].reshape(SLOTS, KVH, HD)
        values_back = kv_back[:, kv_width:].reshape(SLOTS, KVH, HD)
        prob_grad = jnp.einsum(
            "skgh,tkh->kgst", mixed_grad, values_back, preferred_element_type=jnp.float32
        )
        score_grad = (probs * (prob_grad - jnp.sum(probs * prob_grad, -1, keepdims=True))).astype(
            jnp.bfloat16
        )
        query_rot_grad = (
            jnp.einsum(
                "kgst,tkh->skgh", score_grad, keys_back, preferred_element_type=jnp.float32
            ).reshape(seq_len, HQ, HD)
            * scaling
        )
        key_grad_all = (
            jnp.einsum("kgst,skgh->tkh", score_grad, grouped, preferred_element_type=jnp.float32)
            * scaling
        )
        value_grad_all = jnp.einsum(
            "kgst,skgh->tkh",
            probs.astype(jnp.bfloat16),
            mixed_grad,
            preferred_element_type=jnp.float32,
        )
        kv_grad_whole = jnp.concatenate(
            [key_grad_all.reshape(SLOTS, kv_width), value_grad_all.reshape(SLOTS, kv_width)], -1
        )
        kv_grad_local = lax.psum_scatter(
            kv_grad_whole.astype(jnp.bfloat16), "ctx", scatter_dimension=0, tiled=True
        ).astype(jnp.float32)
        key_rot_grad = kv_grad_local[:, :kv_width].reshape(seq_len, KVH, HD)
        value_grad = kv_grad_local[:, kv_width:].astype(jnp.bfloat16)
        query_norm_grad = rotate_back(query_rot_grad, cosine_table, sine_table)
        grad_query_gain = grad_query_gain + jnp.sum(query_norm_grad * query_unit, (0, 1))
        query_grad = (
            norm_back(query_norm_grad * query_gain, query_unit, query_inv)
            .reshape(seq_len, q_width)
            .astype(jnp.bfloat16)
        )
        key_norm_grad = rotate_back(key_rot_grad, cosine_table, sine_table)
        grad_key_gain = grad_key_gain + jnp.sum(key_norm_grad * key_unit, (0, 1))
        key_grad = (
            norm_back(key_norm_grad * key_gain, key_unit, key_inv)
            .reshape(seq_len, kv_width)
            .astype(jnp.bfloat16)
        )
        normed_grad = (
            contract_last(query_grad, mat_query)
            + contract_last(key_grad, mat_key)
            + contract_last(value_grad, mat_value)
        )
        grad_attn_gain = grad_attn_gain + jnp.sum(normed_grad * unit_one, 0)
        input_grads.append(
            (middle_grad + norm_back(normed_grad * attn_gain, unit_one, inv_one)).astype(
                jnp.bfloat16
            )
        )
        stored["normed"].append(normed_bf)
        stored["query"].append(query_grad)
        stored["key"].append(key_grad)
        stored["value"].append(value_grad)
        stored["mixed"].append(mixed_bf)
        stored["attn"].append(attn_grad)
        stored["normed_two"].append(normed_two_bf)
        stored["gate"].append(gate_grad)
        stored["upper"].append(up_grad)
        stored["hidden"].append(hidden_bf)
        stored["branch"].append(branch_grad)
    joined = {name_key: jnp.concatenate(stored[name_key], 0) for name_key in stored}
    right_parts = (
        lax.all_to_all(joined["query"], "ctx", split_axis=1, concat_axis=0, tiled=True),
        lax.all_to_all(joined["key"], "ctx", split_axis=1, concat_axis=0, tiled=True),
        lax.all_to_all(joined["value"], "ctx", split_axis=1, concat_axis=0, tiled=True),
        lax.all_to_all(joined["mixed"], "ctx", split_axis=1, concat_axis=0, tiled=True),
        lax.all_to_all(joined["gate"], "ctx", split_axis=1, concat_axis=0, tiled=True),
        lax.all_to_all(joined["upper"], "ctx", split_axis=1, concat_axis=0, tiled=True),
        lax.all_to_all(joined["hidden"], "ctx", split_axis=1, concat_axis=0, tiled=True),
    )
    left_parts = (
        lax.all_gather(joined["normed"], "ctx", axis=0, tiled=True),
        lax.all_gather(joined["attn"], "ctx", axis=0, tiled=True),
        lax.all_gather(joined["normed_two"], "ctx", axis=0, tiled=True),
        lax.all_gather(joined["branch"], "ctx", axis=0, tiled=True),
    )
    widths = [part.shape[1] for part in right_parts]
    normed_cut = left_parts[0]
    attn_cut = left_parts[1]
    normed_two_cut = left_parts[2]
    branch_cut = left_parts[3]
    block_sums = lax.psum_scatter(
        jnp.concatenate(
            [
                contract_rows(normed_cut, right_parts[0]),
                contract_rows(normed_cut, right_parts[1]),
                contract_rows(normed_cut, right_parts[2]),
                contract_rows(attn_cut, right_parts[3]),
                contract_rows(normed_two_cut, right_parts[4]),
                contract_rows(normed_two_cut, right_parts[5]),
                contract_rows(branch_cut, right_parts[6]),
            ],
            1,
        ).astype(jnp.bfloat16),
        "dp",
        scatter_dimension=0,
        tiled=True,
    ).astype(jnp.float32)
    owned = []
    offset = 0
    for width_now in widths:
        owned.append(block_sums[:, offset : offset + width_now])
        offset = offset + width_now
    gain_totals = lax.psum(
        (grad_attn_gain, grad_query_gain, grad_key_gain, grad_ffn_gain), ("dp", "ctx")
    )
    return (
        jnp.stack(out_rows, 0),
        jnp.stack(input_grads, 0),
        gain_totals[0],
        owned[0],
        owned[1],
        owned[2],
        gain_totals[1],
        gain_totals[2],
        owned[3],
        gain_totals[3],
        owned[4],
        owned[5],
        owned[6],
    )


def solution(mesh):
    in_specs = (
        P("dp", "ctx", None),
        P("dp"),
        P(),
        P("dp", "ctx"),
        P("dp", "ctx"),
        P("dp", "ctx"),
        P(),
        P(),
        P("dp", "ctx"),
        P(),
        P("dp", "ctx"),
        P("dp", "ctx"),
        P("dp", "ctx"),
        P("dp", "ctx", None),
    )
    out_specs = (
        P("dp", "ctx", None),
        P("dp", "ctx", None),
        P(),
        P("dp", "ctx"),
        P("dp", "ctx"),
        P("dp", "ctx"),
        P(),
        P(),
        P("dp", "ctx"),
        P(),
        P("dp", "ctx"),
        P("dp", "ctx"),
        P("dp", "ctx"),
    )
    return jax.shard_map(
        per_device, mesh=mesh, in_specs=in_specs, out_specs=out_specs, check_vma=False
    )
```

profile of v0, /device:TPU:0, one launch (start us, length us, event | category | flops | bytes accessed | tf_op | source)
XLA Modules:
  0.0 2606.6 jit_solution(15764828685533548878)
XLA Ops:
  7.2 8.6 all_gather.62
  15.9 6.3 all_gather.64
  27.6 31.1 %all-gather.17.cloned.1.call-done = bf16[2048,320]{0,1:T(8,128)(2,1)} async-done(((bf16[256,320]{0,1:T(8,128)(2,1)}), bf16[2048,320]{0,1:T(8,128)(2,1)}) %all-gather.17.cloned.1.call-update) | async-done | bytes 1310736 | tf_op jit(solution)/shard_map/all_gather | solution.py:126
  63.0 38.7 %all-gather.19.cloned.1.call-done = bf16[2048,320]{0,1:T(8,128)(2,1)} async-done(((bf16[256,320]{0,1:T(8,128)(2,1)}), bf16[2048,320]{0,1:T(8,128)(2,1)}) %all-gather.19.cloned.1.call-update) | async-done | bytes 1310736 | tf_op jit(solution)/shard_map/all_gather | solution.py:127
  107.5 11.5 all_gather.67
  119.1 12.3 all_gather.69
  133.6 25.2 all-gather.31.cloned.1.call-done
  158.9 26.9 %all-gather.35.cloned.1.call-done = bf16[256,5120]{1,0:T(8,128)(2,1)} async-done(((bf16[256,1280]{1,0:T(8,128)(2,1)}), bf16[256,5120]{1,0:T(8,128)(2,1)}) %all-gather.35.cloned.1.call-update) | async-done | bytes 2621456 | tf_op jit(solution)/shard_map/all_gather | solution.py:122
  194.1 12.0 all-gather.21.cloned.1.call-done
  208.7 18.0 all-gather.39.cloned.1.call-done
  229.1 86.9 %all-gather.23.cloned.1.call-done = bf16[2048,1280]{0,1:T(8,128)(2,1)} async-done(((bf16[256,1280]{0,1:T(8,128)(2,1)}), bf16[2048,1280]{0,1:T(8,128)(2,1)}) %all-gather.23.cloned.1.call-update) | async-done | bytes 5242896 | tf_op jit(solution)/shard_map/all_gather | solution.py:125
  315.9 4.3 multiply_reduce_fusion.10
  328.0 4.6 exponential_reduce_fusion.1
  335.0 6.9 convolution_convert_fusion.10
  341.8 61.6 %all-gather.25.cloned.1.call-done = bf16[2048,1280]{0,1:T(8,128)(2,1)} async-done(((bf16[256,1280]{0,1:T(8,128)(2,1)}), bf16[2048,1280]{0,1:T(8,128)(2,1)}) %all-gather.25.cloned.1.call-update) | async-done | bytes 5242896 | tf_op jit(solution)/shard_map/all_gather | solution.py:128
  403.4 6.0 multiply_reduce_fusion.5
  412.5 4.6 exponential_reduce_fusion
  419.6 6.5 convolution_convert_fusion.9
  426.1 6.0 multiply_reduce_fusion.4
  432.4 372.4 %all-gather.29.cloned.1.call-done = bf16[2048,5120]{1,0:T(8,128)(2,1)} async-done(((bf16[256,5120]{1,0:T(8,128)(2,1)}), bf16[2048,5120]{1,0:T(8,128)(2,1)}) %all-gather.29.cloned.1.call-update) | async-done | bytes 20971536 | tf_op jit(solution)/shard_map/all_gather | solution.py:129
  804.8 12.2 fusion.124
  817.0 391.2 %all-gather.33.cloned.1.call-done = bf16[2048,5120]{1,0:T(8,128)(2,1)} async-done(((bf16[256,5120]{1,0:T(8,128)(2,1)}), bf16[2048,5120]{1,0:T(8,128)(2,1)}) %all-gather.33.cloned.1.call-update) | async-done | bytes 20971536 | tf_op jit(solution)/shard_map/all_gather | solution.py:130
  1208.1 12.4 fusion.125
  1220.5 390.8 %all-gather.37.cloned.1.call-done = bf16[2048,5120]{1,0:T(8,128)(2,1)} async-done(((bf16[256,5120]{1,0:T(8,128)(2,1)}), bf16[2048,5120]{1,0:T(8,128)(2,1)}) %all-gather.37.cloned.1.call-update) | async-done | bytes 20971536 | tf_op jit(solution)/shard_map/all_gather | solution.py:131
  1611.3 15.4 multiply_convert_fusion.2
  1626.7 12.3 fusion.128
  1639.0 13.8 multiply_reduce_fusion.1
  1652.8 12.6 fusion.127
  1665.4 12.3 fusion.126
  1677.6 18.6 multiply_convert_fusion
  1696.3 12.2 fusion.131
  1708.5 14.2 multiply_reduce_fusion
  1722.7 5.7 fusion.108
  1728.4 4.1 convolution_convert_fusion.6
  1732.8 9.5 fusion.67
  1742.3 14.0 fusion.3
  1756.4 14.6 fusion.5
  1776.5 5.0 convolution_convert_fusion.5
  1782.9 14.4 fusion
  1797.2 14.5 fusion.2
  1811.8 3.9 copy-done.3
  1819.0 9.5 fusion.68
  1842.9 6.1 fusion.132
  1849.1 5.9 fusion.129
  1875.8 23.8 all-to-all-done
  1899.6 4.1 all-to-all-start.2
  1906.7 7.7 all-to-all-done.2
  1923.4 4.9 all-to-all-done.1
  1929.0 5.1 all-to-all-start.4
  1942.9 92.3 %all-to-all-done.4 = bf16[512,4,1280]{2,0,1:T(8,128)(2,1)} async-done(((bf16[512,4,1280]{2,0,1:T(8,128)(2,1)}), bf16[512,4,1280]{2,0,1:T(8,128)(2,1)}, u32[]{:S(2)}, u32[]{:S(2)}) %all-to-all-start.4) | async-done | bytes 5242912 | tf_op jit(solution)/shard_map/all_to_all | solution.py:268
  2035.1 5.5 all-to-all-start.5
  2048.0 7.7 fusion.18
  2061.5 7.4 fusion.17
  2068.9 74.9 %all-to-all-done.5 = bf16[512,4,1280]{2,0,1:T(8,128)(2,1)} async-done(((bf16[512,4,1280]{2,0,1:T(8,128)(2,1)}), bf16[512,4,1280]{2,0,1:T(8,128)(2,1)}, u32[]{:S(2)}, u32[]{:S(2)}) %all-to-all-start.5) | async-done | bytes 5242912 | tf_op jit(solution)/shard_map/all_to_all | solution.py:269
  2143.8 5.0 all-to-all-start.6
  2148.9 16.9 fusion.12
  2165.8 15.2 fusion.11
  2181.1 70.0 %all-gather.47.cloned.1.call-done = bf16[2048,2048]{1,0:T(8,128)(2,1)} async-done(((bf16[512,2048]{1,0:T(8,128)(2,1)}), bf16[2048,2048]{1,0:T(8,128)(2,1)}) %all-gather.47.cloned.1.call-update) | async-done | bytes 8388624 | tf_op jit(solution)/shard_map/all_gather | solution.py:276
  2253.3 16.8 fusion.10
  2271.7 12.4 fusion.36
  2284.1 12.5 fusion.35
  2309.8 44.0 %all-reduce = (f32[2048]{0:T(1024)}, f32[64]{0:T(128)}, f32[64]{0:T(128)}, f32[2048]{0:T(1024)}) all-reduce(f32[2048]{0:T(1024)S(1)} %add.241, f32[64]{0:T(128)S(1)} %add.242, f32[64]{0:T(128)S(1)} %add.243, f32[2048]{0:T(1024)S(1)} %add.244), channel_id=1, replica_groups=mesh['dp'=8,'ctx'=4] {'dp','ctx'}, use_global_device_ids=true, to_apply=%region_26.27 | all-reduce | flops 4224 | bytes 33792 | tf_op jit(solution)/shard_map/psum | solution.py:305
  2353.8 4.7 fusion.76
  2360.0 227.7 %reduce-scatter.8.cloned.1.call-done = bf16[256,4640]{0,1:T(8,128)(2,1)} async-done(((bf16[2048,4640]{0,1:T(8,128)(2,1)}), bf16[256,4640]{0,1:T(8,128)(2,1)}) %reduce-scatter.8.cloned.1.call-update) | async-done | bytes 2375696 | tf_op jit(solution)/shard_map/reduce_scatter | solution.py:283
  (376 shorter events, 156.7 us)
Async XLA Ops:
  7.2 18.5 copy-start.6
  7.2 19.0 copy-start.87
  7.2 51.5 %all-gather.17.cloned.1.call-start = ((), (), s32[]{:S(2)}) async-start(), calls=%async_computation.10 | async-start | bytes 1474560 | tf_op jit(solution)/shard_map/all_gather | solution.py:126
  15.9 85.8 %all-gather.19.cloned.1.call-start = ((), (), s32[]{:S(2)}) async-start(), calls=%async_computation.11 | async-start | bytes 1474560 | tf_op jit(solution)/shard_map/all_gather | solution.py:127
  22.2 111.3 %all-gather.27.cloned.1.call-start = ((), (), s32[]{:S(2)}) async-start(), calls=%async_computation.15 | async-start | bytes 3276800 | tf_op jit(solution)/shard_map/all_gather | solution.py:120
  23.0 135.8 %all-gather.31.cloned.1.call-start = ((), (), s32[]{:S(2)}) async-start(), calls=%async_computation.17 | async-start | bytes 3276800 | tf_op jit(solution)/shard_map/all_gather | solution.py:121
  23.5 162.2 %all-gather.35.cloned.1.call-start = ((), (), s32[]{:S(2)}) async-start(), calls=%async_computation.19 | async-start | bytes 3276800 | tf_op jit(solution)/shard_map/all_gather | solution.py:122
  24.1 182.0 %all-gather.21.cloned.1.call-start = ((), (), s32[]{:S(2)}) async-start(), calls=%async_computation.12 | async-start | bytes 1638400 | tf_op jit(solution)/shard_map/all_gather | solution.py:153
  25.1 298.3 %copy-start.51 = (f32[256,64]{0,1:T(8,128)}, f32[256,64]{0,1:T(8,128)S(1)}, u32[]{:S(2)}) copy-start(f32[256,64]{0,1:T(8,128)S(1)} %get-tuple-element.156) | copy-start | bytes 196612
  25.7 297.7 %copy-start.63 = (f32[256,64]{0,1:T(8,128)}, f32[256,64]{0,1:T(8,128)S(1)}, u32[]{:S(2)}) copy-start(f32[256,64]{0,1:T(8,128)S(1)} %get-tuple-element.158) | copy-start | bytes 196612
  26.2 289.7 %copy-start.95 = (f32[256]{0:T(256)}, f32[256]{0:T(256)S(1)}, u32[]{:S(2)}) copy-start(f32[256]{0:T(256)S(1)} %get-tuple-element.195) | copy-start | bytes 3076
  26.2 294.1 %copy-start.97 = (f32[256]{0:T(256)}, f32[256]{0:T(256)S(1)}, u32[]{:S(2)}) copy-start(f32[256]{0:T(256)S(1)} %get-tuple-element.196) | copy-start | bytes 3076
  27.6 74.1 %copy-start.41 = (bf16[256,2048]{1,0:T(8,128)(2,1)}, bf16[256,2048]{1,0:T(8,128)(2,1)S(1)}, u32[]{:S(2)}) copy-start(bf16[256,2048]{1,0:T(8,128)(2,1)S(1)} %get-tuple-element.114) | copy-start | bytes 3145732
  104.4 14.7 copy-start.81
  104.4 122.2 %all-gather.39.cloned.1.call-start = ((), (), s32[]{:S(2)}) async-start(), calls=%async_computation.21 | async-start | bytes 1638400 | tf_op jit(solution)/shard_map/all_gather | solution.py:153
  107.4 208.5 %all-gather.23.cloned.1.call-start = ((), (), s32[]{:S(2)}) async-start(), calls=%async_computation.13 | async-start | bytes 5898240 | tf_op jit(solution)/shard_map/all_gather | solution.py:125
  119.0 284.4 %all-gather.25.cloned.1.call-start = ((), (), s32[]{:S(2)}) async-start(), calls=%async_computation.14 | async-start | bytes 5898240 | tf_op jit(solution)/shard_map/all_gather | solution.py:128
  131.5 673.3 %all-gather.29.cloned.1.call-start = ((), (), s32[]{:S(2)}) async-start(), calls=%async_computation.16 | async-start | bytes 23592960 | tf_op jit(solution)/shard_map/all_gather | solution.py:129
  133.6 1074.6 %all-gather.33.cloned.1.call-start = ((), (), s32[]{:S(2)}) async-start(), calls=%async_computation.18 | async-start | bytes 23592960 | tf_op jit(solution)/shard_map/all_gather | solution.py:130
  158.8 27.3 %copy-start.105 = (s32[2]{0:T(128)S(1)}, s32[2]{0:T(128)}, u32[]{:S(2)}) copy-start(s32[2]{0:T(128)} %param.15) | copy-start | bytes 28
  158.8 1452.5 %all-gather.37.cloned.1.call-start = ((), (), s32[]{:S(2)}) async-start(), calls=%async_computation.20 | async-start | bytes 23592960 | tf_op jit(solution)/shard_map/all_gather | solution.py:131
  185.8 1675.9 %reduce-scatter.4.cloned.1.call-start = ((), (), s32[]{:S(2)}) async-start(), calls=%async_computation.22 | async-start | bytes 1638400 | tf_op jit(solution)/shard_map/reduce_scatter | solution.py:221
  189.3 19.4 copy-start.89
  189.3 19.4 copy-start.92
  328.0 7.0 copy-start.1
  332.6 9.2 copy-start.76
  412.5 7.1 copy-start
  417.1 9.0 copy-start.74
  432.4 775.8 %copy-start.39 = (bf16[256,2048]{1,0:T(8,128)(2,1)}, bf16[256,2048]{1,0:T(8,128)(2,1)S(1)}, u32[]{:S(2)}) copy-start(bf16[256,2048]{1,0:T(8,128)(2,1)S(1)} %multiply_convert_fusion.7) | copy-start | bytes 3145732
  1626.7 12.3 copy-start.48
  1652.8 12.6 copy-start.65
  1665.4 12.3 copy-start.40
  1696.3 12.2 copy-start.49
  1708.5 14.2 copy-start.90
  1708.5 14.2 copy-start.93
  1732.8 9.6 copy-start.34
  1756.4 14.6 copy-start.26
  1776.1 87.6 %reduce-scatter.6.cloned.1.call-start = ((), (), s32[]{:S(2)}) async-start(), calls=%async_computation.23 | async-start | bytes 1638400 | tf_op jit(solution)/shard_map/reduce_scatter | solution.py:221
  1797.2 18.5 copy-start.24
  1829.6 218.3 %all-gather.41.cloned.1.call-start = ((), (), s32[]{:S(2)}) async-start(), calls=%async_computation.24 | async-start | bytes 10485760 | tf_op jit(solution)/shard_map/all_gather | solution.py:273
  1832.9 228.5 %all-gather.43.cloned.1.call-start = ((), (), s32[]{:S(2)}) async-start(), calls=%async_computation.25 | async-start | bytes 10485760 | tf_op jit(solution)/shard_map/all_gather | solution.py:274
  1834.5 314.4 %all-gather.45.cloned.1.call-start = ((), (), s32[]{:S(2)}) async-start(), calls=%async_computation.26 | async-start | bytes 10485760 | tf_op jit(solution)/shard_map/all_gather | solution.py:275
  1839.2 28.0 %all-to-all-start.3 = ((bf16[512,4,320]{0,2,1:T(8,128)(2,1)}), bf16[512,4,320]{0,2,1:T(8,128)(2,1)S(1)}, u32[]{:S(2)}, u32[]{:S(2)}) async-start(bf16[512,4,320]{0,2,1:T(8,128)(2,1)} %pad_maximum_fusion.12), calls=%async_computation.5 | async-start | bytes 2621440 | tf_op jit(solution)/shard_map/all_to_all | solution.py:267
  1865.3 8.3 copy-start.44
  1865.3 8.3 copy-start.46
  1865.4 8.3 copy-start.52
  1865.4 8.3 copy-start.83
  1865.4 8.3 copy-start.85
  1865.4 8.3 copy-start.102
  1867.2 32.4 %all-to-all-start = ((bf16[512,4,320]{0,2,1:T(8,128)(2,1)}), bf16[512,4,320]{0,2,1:T(8,128)(2,1)S(1)}, u32[]{:S(2)}, u32[]{:S(2)}) async-start(bf16[512,4,320]{0,2,1:T(8,128)(2,1)} %pad_maximum_fusion.11), calls=%async_computation.2 | async-start | bytes 2621440 | tf_op jit(solution)/shard_map/all_to_all | solution.py:264
  1899.6 14.7 all-to-all-start.2
  1914.3 14.0 all-to-all-start.1
  1929.0 106.1 %all-to-all-start.4 = ((bf16[512,4,1280]{2,0,1:T(8,128)(2,1)}), bf16[512,4,1280]{2,0,1:T(8,128)(2,1)}, u32[]{:S(2)}, u32[]{:S(2)}) async-start(bf16[512,4,1280]{2,0,1:T(8,128)(2,1)} %bitcast.382), calls=%async_computation.6 | async-start | bytes 10485760 | tf_op jit(solution)/shard_map/all_to_all | solution.py:268
  1934.1 317.0 %all-gather.47.cloned.1.call-start = ((), (), s32[]{:S(2)}) async-start(), calls=%async_computation.27 | async-start | bytes 10485760 | tf_op jit(solution)/shard_map/all_gather | solution.py:276
  2035.1 108.7 %all-to-all-start.5 = ((bf16[512,4,1280]{2,0,1:T(8,128)(2,1)}), bf16[512,4,1280]{2,0,1:T(8,128)(2,1)}, u32[]{:S(2)}, u32[]{:S(2)}) async-start(bf16[512,4,1280]{2,0,1:T(8,128)(2,1)} %bitcast.381), calls=%async_computation.7 | async-start | bytes 10485760 | tf_op jit(solution)/shard_map/all_to_all | solution.py:269
  2048.0 8.8 copy-start.61
  2048.0 8.9 copy-start.4
  2143.8 109.5 %all-to-all-start.6 = ((bf16[512,4,1280]{2,0,1:T(8,128)(2,1)}), bf16[512,4,1280]{2,0,1:T(8,128)(2,1)}, u32[]{:S(2)}, u32[]{:S(2)}) async-start(bf16[512,4,1280]{2,0,1:T(8,128)(2,1)} %bitcast.380), calls=%async_computation.8 | async-start | bytes 10485760 | tf_op jit(solution)/shard_map/all_to_all | solution.py:270
  2148.9 438.9 %reduce-scatter.8.cloned.1.call-start = ((), (), s32[]{:S(2)}) async-start(), calls=%async_computation.28 | async-start | bytes 21381120 | tf_op jit(solution)/shard_map/reduce_scatter | solution.py:283
  2148.9 16.9 copy-start.108
  2271.7 12.4 copy-start.91
  2271.7 27.8 %slice-start = ((s8[5242880]{0:T(1024)(128)(4,1)}), s8[4194304]{0:T(1024)(128)(4,1)S(1)}, s32[]{:S(2)}) async-start(s8[5242880]{0:T(1024)(128)(4,1)} %bitcast.378), calls=%async_computation.29 | async-start | bytes 8388608
  2284.1 12.5 copy-start.66
  2284.1 15.4 slice-start.1
  (73 other events, 187.2 us)
Sparse Core Ops, SparseCore 0:
  16.0 42.6 all-gather.16
  60.8 40.9 all-gather.18
  103.3 30.2 all-gather.26
  135.0 23.7 all-gather.30
  160.2 25.5 all-gather.34
  187.8 18.3 all-gather.20
  208.3 18.3 all-gather.38
  228.7 87.1 all-gather.22
  318.0 85.3 all-gather.24
  404.8 399.9 all-gather.28
  806.3 401.7 all-gather.32
  1209.5 401.7 all-gather.36
  1776.2 26.5 reduce-scatter.3
  1829.7 33.8 reduce-scatter.5
  1865.1 79.0 all-gather.40
  1945.6 98.5 all-gather.42
  2045.6 101.1 all-gather.44
  2148.2 102.8 all-gather.46
  2270.2 317.4 reduce-scatter.7
where the time goes:
time: 2610 us
  waiting for transfers between devices  1960 us (75%)
  matrix products  356 us (14%)
  other arithmetic  104 us (4%)
  blocking collectives  82.8 us (3%)
  local copies, waits for them, and re-layouts  53.4 us (2%)
  starting transfers between devices  31.4 us (1%)
    all_gather x1, waiting for transfers between devices, per_device(): lax.all_gather(columns[5], 'dp', axis=0, tiled=True)  391 us
    all_gather x1, waiting for transfers between devices, per_device(): lax.all_gather(columns[6], 'dp', axis=0, tiled=True)  391 us
    all_gather x1, waiting for transfers between devices, per_device(): lax.all_gather(columns[4], 'dp', axis=0, tiled=True)  372 us
    reduce_scatter x1, waiting for transfers between devices, per_device(): lax.psum_scatter(jnp.concatenate([contract_rows(normed_cut, right_parts[0...  228 us
    dot_general x14, matrix products, contract_last(): lax.dot_general(left_side, right_side, (((1,), (1,)), ((), ())), preferre...  97.2 us
    all_to_all x1, waiting for transfers between devices, per_device(): lax.all_to_all(joined['gate'], 'ctx', split_axis=1, concat_axis=0, tiled=...  92.3 us
    all_gather x1, waiting for transfers between devices, per_device(): lax.all_gather(columns[0], 'dp', axis=0, tiled=True)  86.9 us
    all_to_all x1, waiting for transfers between devices, per_device(): lax.all_to_all(joined['upper'], 'ctx', split_axis=1, concat_axis=0, tiled...  74.9 us
  transfers between devices with their start and end apart: 26, of which 22 were waited for; matrix products, arithmetic and copies ran while one was open for 12% of the time, Pallas kernels for 0%

commit v1 on v0

--- a/solution.py
+++ b/solution.py
@@ -11,6 +11,24 @@
 SLOTS = 1024
 EPSILON = 1e-06
 ROPE_BASE = 10000.0
+
+
+def collect(shard, axis, dim):
+    ways, here, step = (lax.axis_size(axis), lax.axis_index(axis), shard.shape[dim])
+    lengths = [n * ways if d == dim else n for d, n in enumerate(shard.shape)]
+    full = lax.dynamic_update_slice_in_dim(
+        jnp.zeros(lengths, shard.dtype), shard, here * step, axis=dim
+    )
+    going_up = going_down = shard
+    for far in range(1, ways // 2 + 1):
+        going_up = lax.ppermute(going_up, axis, [(d, (d + 1) % ways) for d in range(ways)])
+        full = lax.dynamic_update_slice_in_dim(full, going_up, (here - far) % ways * step, axis=dim)
+        if 2 * far < ways:
+            going_down = lax.ppermute(going_down, axis, [(d, (d - 1) % ways) for d in range(ways)])
+            full = lax.dynamic_update_slice_in_dim(
+                full, going_down, (here + far) % ways * step, axis=dim
+            )
+    return full
 
 
 def norm_rows(values, gain_vec):
@@ -127,7 +145,7 @@
         lax.all_gather(columns[2], "dp", axis=0, tiled=True),
         lax.all_gather(columns[3], "dp", axis=0, tiled=True),
         lax.all_gather(columns[4], "dp", axis=0, tiled=True),
-        lax.all_gather(columns[5], "dp", axis=0, tiled=True),
+        collect(columns[5], "dp", 0),
         lax.all_gather(columns[6], "dp", axis=0, tiled=True),
     )
     for batch_index in range(micro_count):

time: 2610 us -> 2520 us (0.966)
  waiting for transfers between devices: 1960 us -> 1810 us
  local copies, waits for them, and re-layouts: 53.4 us -> 82.2 us
    all_gather x1 -> x0, waiting for transfers between devices: 391 us -> none  [per_device(): lax.all_gather(columns[5], 'dp', axis=0, tiled=True)]
    ppermute x0 -> x7, waiting for transfers between devices: none -> 349 us  [the longest x4 265 us: collect(): lax.ppermute(going_up, axis, [(d, (d + 1) % ways) for d in range(ways)])]
    all_gather x1, waiting for transfers between devices: 86.9 us -> 0.01 us  [per_device(): lax.all_gather(columns[0], 'dp', axis=0, tiled=True)]
    all_gather x2, waiting for transfers between devices: 30 us -> 0.01 us  [per_device(): kv_whole = lax.all_gather(kv_local, 'ctx', axis=0, tiled=True)]
  transfers between devices with their start and end apart: 26 -> 32, of which waited for: 22 -> 23; matrix products, arithmetic and copies ran while one was open for 12% -> 13% of each run, Pallas kernels for 0% -> 0%
where the time goes in v1:
time: 2520 us; the launch traced here: 2510 us
  waiting for transfers between devices  1810 us (72%)
  matrix products  363 us (14%)
  other arithmetic  106 us (4%)
  blocking collectives  82.9 us (3%)
  local copies, waits for them, and re-layouts  82.2 us (3%)
  starting transfers between devices  49 us (2%)
    all_gather x1, waiting for transfers between devices, per_device(): lax.all_gather(columns[6], 'dp', axis=0, tiled=True)  396 us
    all_gather x1, waiting for transfers between devices, per_device(): lax.all_gather(columns[4], 'dp', axis=0, tiled=True)  363 us
    ppermute x4, waiting for transfers between devices, collect(): lax.ppermute(going_up, axis, [(d, (d + 1) % ways) for d in range(ways)])  265 us
    reduce_scatter x1, waiting for transfers between devices, per_device(): lax.psum_scatter(jnp.concatenate([contract_rows(normed_cut, right_parts[0...  227 us
    dot_general x14, matrix products, contract_last(): lax.dot_general(left_side, right_side, (((1,), (1,)), ((), ())), preferre...  92.3 us
    all_to_all x1, waiting for transfers between devices, per_device(): lax.all_to_all(joined['upper'], 'ctx', split_axis=1, concat_axis=0, tiled...  92.2 us
    ppermute x3, waiting for transfers between devices, collect(): lax.ppermute(going_down, axis, [(d, (d - 1) % ways) for d in range(ways)])  84.3 us
    all_to_all x1, waiting for transfers between devices, per_device(): lax.all_to_all(joined['gate'], 'ctx', split_axis=1, concat_axis=0, tiled=...  75 us
  transfers between devices with their start and end apart: 32, of which 23 were waited for; matrix products, arithmetic and copies ran while one was open for 13% of the time, Pallas kernels for 0%

profile of v1, /device:TPU:0, one launch (start us, length us, event | category | flops | bytes accessed | tf_op | source)
XLA Modules:
  0.0 2506.8 jit_solution(14548081393175535532)
XLA Ops:
  7.2 8.6 all_gather.59
  15.9 6.3 all_gather.61
  27.6 31.1 %all-gather.16.cloned.1.call-done = bf16[2048,320]{0,1:T(8,128)(2,1)} async-done(((bf16[256,320]{0,1:T(8,128)(2,1)}), bf16[2048,320]{0,1:T(8,128)(2,1)}) %all-gather.16.cloned.1.call-update) | async-done | bytes 1310736 | tf_op jit(solution)/shard_map/all_gather | solution.py:144
  63.0 38.7 %all-gather.18.cloned.1.call-done = bf16[2048,320]{0,1:T(8,128)(2,1)} async-done(((bf16[256,320]{0,1:T(8,128)(2,1)}), bf16[2048,320]{0,1:T(8,128)(2,1)}) %all-gather.18.cloned.1.call-update) | async-done | bytes 1310736 | tf_op jit(solution)/shard_map/all_gather | solution.py:145
  107.5 11.5 all_gather.64
  119.1 12.3 all_gather.66
  133.6 25.2 %all-gather.32.cloned.1.call-done = bf16[256,5120]{1,0:T(8,128)(2,1)} async-done(((bf16[256,1280]{1,0:T(8,128)(2,1)}), bf16[256,5120]{1,0:T(8,128)(2,1)}) %all-gather.32.cloned.1.call-update) | async-done | bytes 2621456 | tf_op jit(solution)/shard_map/all_gather | solution.py:140
  158.9 26.9 %all-gather.30.cloned.1.call-done = bf16[256,5120]{1,0:T(8,128)(2,1)} async-done(((bf16[256,1280]{1,0:T(8,128)(2,1)}), bf16[256,5120]{1,0:T(8,128)(2,1)}) %all-gather.30.cloned.1.call-update) | async-done | bytes 2621456 | tf_op jit(solution)/shard_map/all_gather | solution.py:139
  197.2 134.3 %collective-permute-done = bf16[256,5120]{1,0:T(8,128)(2,1)} collective-permute-done((bf16[256,5120]{1,0:T(8,128)(2,1)}, bf16[256,5120]{1,0:T(8,128)(2,1)}, u32[]{:S(2)}, u32[]{:S(2)}) %collective-permute-start) | collective-permute-done | bytes 2621472 | tf_op jit(solution)/shard_map/ppermute | solution.py:24
  337.9 7.4 broadcast_in_dim.20
  358.7 96.1 %collective-permute-done.2 = bf16[256,5120]{1,0:T(8,128)(2,1)} collective-permute-done((bf16[256,5120]{1,0:T(8,128)(2,1)}, bf16[256,5120]{1,0:T(8,128)(2,1)}, u32[]{:S(2)}, u32[]{:S(2)}) %collective-permute-start.2) | collective-permute-done | bytes 2621472 | tf_op jit(solution)/shard_map/ppermute | solution.py:24
  467.1 4.4 multiply_reduce_fusion.10
  479.1 5.0 exponential_reduce_fusion.1
  486.3 4.6 fusion.9
  491.0 6.1 exponential_reduce_fusion
  497.0 13.5 convolution_convert_fusion.10
  511.3 6.5 convolution_convert_fusion.9
  517.8 70.7 %all-gather.24.cloned.1.call-done = bf16[2048,1280]{0,1:T(8,128)(2,1)} async-done(((bf16[256,1280]{0,1:T(8,128)(2,1)}), bf16[2048,1280]{0,1:T(8,128)(2,1)}) %all-gather.24.cloned.1.call-update) | async-done | bytes 5242896 | tf_op jit(solution)/shard_map/all_gather | solution.py:146
  588.6 4.8 multiply_reduce_fusion.5
  593.3 34.3 %collective-permute-done.4 = bf16[256,5120]{1,0:T(8,128)(2,1)} collective-permute-done((bf16[256,5120]{1,0:T(8,128)(2,1)}, bf16[256,5120]{1,0:T(8,128)(2,1)}, u32[]{:S(2)}, u32[]{:S(2)}) %collective-permute-start.4) | collective-permute-done | bytes 2621472 | tf_op jit(solution)/shard_map/ppermute | solution.py:24
  637.2 84.2 %collective-permute-done.5 = bf16[256,5120]{1,0:T(8,128)(2,1)} collective-permute-done((bf16[256,5120]{1,0:T(8,128)(2,1)}, bf16[256,5120]{1,0:T(8,128)(2,1)}, u32[]{:S(2)}, u32[]{:S(2)}) %collective-permute-start.5) | collective-permute-done | bytes 2621472 | tf_op jit(solution)/shard_map/ppermute | solution.py:27
  726.5 362.9 %all-gather.28.cloned.1.call-done = bf16[2048,5120]{1,0:T(8,128)(2,1)} async-done(((bf16[256,5120]{1,0:T(8,128)(2,1)}), bf16[2048,5120]{1,0:T(8,128)(2,1)}) %all-gather.28.cloned.1.call-update) | async-done | bytes 20971536 | tf_op jit(solution)/shard_map/all_gather | solution.py:147
  1089.4 12.2 fusion.124
  1101.6 396.1 %all-gather.34.cloned.1.call-done = bf16[2048,5120]{1,0:T(8,128)(2,1)} async-done(((bf16[256,5120]{1,0:T(8,128)(2,1)}), bf16[2048,5120]{1,0:T(8,128)(2,1)}) %all-gather.34.cloned.1.call-update) | async-done | bytes 20971536 | tf_op jit(solution)/shard_map/all_gather | solution.py:149
  1497.7 11.6 fusion.126
  1509.3 18.7 multiply_convert_fusion.2
  1528.0 12.2 fusion.127
  1540.2 13.8 multiply_reduce_fusion.1
  1554.0 12.6 fusion.125
  1566.7 12.2 fusion.130
  1578.9 18.7 multiply_convert_fusion
  1597.5 12.2 fusion.131
  1609.7 13.7 multiply_reduce_fusion
  1623.4 5.7 fusion.108
  1629.2 4.1 convolution_convert_fusion.6
  1633.5 9.5 fusion.67
  1643.1 14.3 fusion.3
  1657.3 14.4 fusion.5
  1677.3 5.0 convolution_convert_fusion.5
  1683.7 14.6 fusion
  1698.2 14.5 fusion.2
  1719.8 9.5 fusion.68
  1743.8 6.1 fusion.132
  1749.9 5.9 fusion.128
  1776.7 23.1 all-to-all-done
  1799.8 4.1 all-to-all-start.2
  1806.9 7.7 all-to-all-done.2
  1823.5 5.0 all-to-all-done.1
  1829.3 5.1 all-to-all-start.5
  1843.2 92.2 %all-to-all-done.5 = bf16[512,4,1280]{2,0,1:T(8,128)(2,1)} async-done(((bf16[512,4,1280]{2,0,1:T(8,128)(2,1)}), bf16[512,4,1280]{2,0,1:T(8,128)(2,1)}, u32[]{:S(2)}, u32[]{:S(2)}) %all-to-all-start.5) | async-done | bytes 5242912 | tf_op jit(solution)/shard_map/all_to_all | solution.py:287
  1935.4 5.5 all-to-all-start.4
  1948.2 7.7 fusion.18
  1961.6 7.4 fusion.17
  1969.0 75.0 %all-to-all-done.4 = bf16[512,4,1280]{2,0,1:T(8,128)(2,1)} async-done(((bf16[512,4,1280]{2,0,1:T(8,128)(2,1)}), bf16[512,4,1280]{2,0,1:T(8,128)(2,1)}, u32[]{:S(2)}, u32[]{:S(2)}) %all-to-all-start.4) | async-done | bytes 5242912 | tf_op jit(solution)/shard_map/all_to_all | solution.py:286
  2044.0 5.0 all-to-all-start.6
  2049.2 16.9 fusion.12
  2066.1 15.2 fusion.11
  2081.3 70.1 %all-gather.44.cloned.1.call-done = bf16[2048,2048]{1,0:T(8,128)(2,1)} async-done(((bf16[512,2048]{1,0:T(8,128)(2,1)}), bf16[2048,2048]{1,0:T(8,128)(2,1)}) %all-gather.44.cloned.1.call-update) | async-done | bytes 8388624 | tf_op jit(solution)/shard_map/all_gather | solution.py:294
  2153.5 16.8 fusion.10
  2171.9 12.4 fusion.36
  2184.4 12.5 fusion.35
  2210.0 44.1 %all-reduce = (f32[2048]{0:T(1024)}, f32[64]{0:T(128)}, f32[64]{0:T(128)}, f32[2048]{0:T(1024)}) all-reduce(f32[2048]{0:T(1024)S(1)} %add.318, f32[64]{0:T(128)S(1)} %add.319, f32[64]{0:T(128)S(1)} %add.320, f32[2048]{0:T(1024)S(1)} %add.321), channel_id=1, replica_groups=mesh['dp'=8,'ctx'=4] {'dp','ctx'}, use_global_device_ids=true, to_apply=%region_26.27 | all-reduce | flops 4224 | bytes 33792 | tf_op jit(solution)/shard_map/psum | solution.py:323
  2254.1 4.7 fusion.76
  2260.3 227.3 %reduce-scatter.8.cloned.1.call-done = bf16[256,4640]{0,1:T(8,128)(2,1)} async-done(((bf16[2048,4640]{0,1:T(8,128)(2,1)}), bf16[256,4640]{0,1:T(8,128)(2,1)}) %reduce-scatter.8.cloned.1.call-update) | async-done | bytes 2375696 | tf_op jit(solution)/shard_map/reduce_scatter | solution.py:301
  (400 shorter events, 199.8 us)
Async XLA Ops:
  7.2 18.5 copy-start.7
  7.2 19.0 copy-start.89
  7.2 51.5 %all-gather.16.cloned.1.call-start = ((), (), s32[]{:S(2)}) async-start(), calls=%async_computation.10 | async-start | bytes 1474560 | tf_op jit(solution)/shard_map/all_gather | solution.py:144
  15.9 85.8 %all-gather.18.cloned.1.call-start = ((), (), s32[]{:S(2)}) async-start(), calls=%async_computation.11 | async-start | bytes 1474560 | tf_op jit(solution)/shard_map/all_gather | solution.py:145
  22.2 111.3 %all-gather.26.cloned.1.call-start = ((), (), s32[]{:S(2)}) async-start(), calls=%async_computation.15 | async-start | bytes 3276800 | tf_op jit(solution)/shard_map/all_gather | solution.py:138
  23.0 135.8 %all-gather.32.cloned.1.call-start = ((), (), s32[]{:S(2)}) async-start(), calls=%async_computation.18 | async-start | bytes 3276800 | tf_op jit(solution)/shard_map/all_gather | solution.py:140
  23.5 162.2 %all-gather.30.cloned.1.call-start = ((), (), s32[]{:S(2)}) async-start(), calls=%async_computation.17 | async-start | bytes 3276800 | tf_op jit(solution)/shard_map/all_gather | solution.py:139
  24.1 322.9 %all-gather.20.cloned.1.call-start = ((), (), s32[]{:S(2)}) async-start(), calls=%async_computation.12 | async-start | bytes 1638400 | tf_op jit(solution)/shard_map/all_gather | solution.py:171
  25.1 449.5 %copy-start.53 = (f32[256,64]{0,1:T(8,128)}, f32[256,64]{0,1:T(8,128)S(1)}, u32[]{:S(2)}) copy-start(f32[256,64]{0,1:T(8,128)S(1)} %get-tuple-element.156) | copy-start | bytes 196612
  25.7 448.8 %copy-start.65 = (f32[256,64]{0,1:T(8,128)}, f32[256,64]{0,1:T(8,128)S(1)}, u32[]{:S(2)}) copy-start(f32[256,64]{0,1:T(8,128)S(1)} %get-tuple-element.158) | copy-start | bytes 196612
  26.2 440.9 %copy-start.97 = (f32[256]{0:T(256)}, f32[256]{0:T(256)S(1)}, u32[]{:S(2)}) copy-start(f32[256]{0:T(256)S(1)} %get-tuple-element.195) | copy-start | bytes 3076
  26.2 445.3 %copy-start.99 = (f32[256]{0:T(256)}, f32[256]{0:T(256)S(1)}, u32[]{:S(2)}) copy-start(f32[256]{0:T(256)S(1)} %get-tuple-element.196) | copy-start | bytes 3076
  27.6 74.1 %copy-start.41 = (bf16[256,2048]{1,0:T(8,128)(2,1)}, bf16[256,2048]{1,0:T(8,128)(2,1)S(1)}, u32[]{:S(2)}) copy-start(bf16[256,2048]{1,0:T(8,128)(2,1)S(1)} %get-tuple-element.114) | copy-start | bytes 3145732
  104.4 14.7 copy-start.83
  104.4 244.8 %all-gather.36.cloned.1.call-start = ((), (), s32[]{:S(2)}) async-start(), calls=%async_computation.20 | async-start | bytes 1638400 | tf_op jit(solution)/shard_map/all_gather | solution.py:171
  107.4 359.7 %all-gather.22.cloned.1.call-start = ((), (), s32[]{:S(2)}) async-start(), calls=%async_computation.13 | async-start | bytes 5898240 | tf_op jit(solution)/shard_map/all_gather | solution.py:143
  119.0 469.5 %all-gather.24.cloned.1.call-start = ((), (), s32[]{:S(2)}) async-start(), calls=%async_computation.14 | async-start | bytes 5898240 | tf_op jit(solution)/shard_map/all_gather | solution.py:146
  131.4 957.9 %all-gather.28.cloned.1.call-start = ((), (), s32[]{:S(2)}) async-start(), calls=%async_computation.16 | async-start | bytes 23592960 | tf_op jit(solution)/shard_map/all_gather | solution.py:147
  133.6 57.0 %copy-start.107 = (s32[2]{0:T(128)S(1)}, s32[2]{0:T(128)}, u32[]{:S(2)}) copy-start(s32[2]{0:T(128)} %param.15) | copy-start | bytes 28
  133.6 1364.1 %all-gather.34.cloned.1.call-start = ((), (), s32[]{:S(2)}) async-start(), calls=%async_computation.19 | async-start | bytes 23592960 | tf_op jit(solution)/shard_map/all_gather | solution.py:149
  158.8 1603.8 %reduce-scatter.4.cloned.1.call-start = ((), (), s32[]{:S(2)}) async-start(), calls=%async_computation.21 | async-start | bytes 1638400 | tf_op jit(solution)/shard_map/reduce_scatter | solution.py:239
  185.8 145.7 %collective-permute-start = (bf16[256,5120]{1,0:T(8,128)(2,1)}, bf16[256,5120]{1,0:T(8,128)(2,1)}, u32[]{:S(2)}, u32[]{:S(2)}) collective-permute-start(bf16[256,5120]{1,0:T(8,128)(2,1)} %all-gather.30.cloned.1.call-done), channel_id=1, source_target_pairs={{0,4},{4,8},{8,12},{12,16},{16,20},{20,24},{24,28},{28,0},{1,5},{5... | collective-permute-start | bytes 7864328 | tf_op jit(solution)/shard_map/ppermute | solution.py:24
  187.3 146.8 %collective-permute-start.1 = (bf16[256,5120]{1,0:T(8,128)(2,1)}, bf16[256,5120]{1,0:T(8,128)(2,1)}, u32[]{:S(2)}, u32[]{:S(2)}) collective-permute-start(bf16[256,5120]{1,0:T(8,128)(2,1)} %all-gather.30.cloned.1.call-done), channel_id=1, source_target_pairs={{0,28},{4,0},{8,4},{12,8},{16,12},{20,16},{24,20},{28,24},{1,29},{... | collective-permute-start | bytes 7864328 | tf_op jit(solution)/shard_map/ppermute | solution.py:27
  193.7 151.6 %copy-start.91 = (f32[256]{0:T(256)}, f32[256]{0:T(256)S(1)}, u32[]{:S(2)}) copy-start(f32[256]{0:T(256)S(1)} %get-tuple-element.197) | copy-start | bytes 3076
  193.7 151.6 %copy-start.94 = (f32[256]{0:T(256)}, f32[256]{0:T(256)S(1)}, u32[]{:S(2)}) copy-start(f32[256]{0:T(256)S(1)} %get-tuple-element.198) | copy-start | bytes 3076
  331.5 123.3 %collective-permute-start.2 = (bf16[256,5120]{1,0:T(8,128)(2,1)}, bf16[256,5120]{1,0:T(8,128)(2,1)}, u32[]{:S(2)}, u32[]{:S(2)}) collective-permute-start(bf16[256,5120]{1,0:T(8,128)(2,1)} %collective-permute-done), channel_id=1, source_target_pairs={{0,4},{4,8},{8,12},{12,16},{16,20},{20,24},{24,28},{28,0},{1,5},{5... | collective-permute-start | bytes 7864328 | tf_op jit(solution)/shard_map/ppermute | solution.py:24
  334.0 123.2 %collective-permute-start.3 = (bf16[256,5120]{1,0:T(8,128)(2,1)}, bf16[256,5120]{1,0:T(8,128)(2,1)}, u32[]{:S(2)}, u32[]{:S(2)}) collective-permute-start(bf16[256,5120]{1,0:T(8,128)(2,1)} %collective-permute-done.1), channel_id=1, source_target_pairs={{0,28},{4,0},{8,4},{12,8},{16,12},{20,16},{24,20},{28,24},{1,29},{... | collective-permute-start | bytes 7864328 | tf_op jit(solution)/shard_map/ppermute | solution.py:27
  337.9 141.3 %copy-start.14 = (pred[256,1024]{0,1:T(8,128)(4,1)}, pred[256,1024]{0,1:T(8,128)(4,1)S(1)}, u32[]{:S(2)}) copy-start(pred[256,1024]{0,1:T(8,128)(4,1)S(1)} %get-tuple-element.162) | copy-start | bytes 786436
  349.2 126.8 %copy-start.28 = (bf16[1024,320]{0,1:T(8,128)(2,1)}, bf16[1024,320]{0,1:T(8,128)(2,1)S(1)}, u32[]{:S(2)}) copy-start(bf16[1024,320]{0,1:T(8,128)(2,1)S(1)} %get-tuple-element.124) | copy-start | bytes 1966084
  454.8 172.8 %collective-permute-start.4 = (bf16[256,5120]{1,0:T(8,128)(2,1)}, bf16[256,5120]{1,0:T(8,128)(2,1)}, u32[]{:S(2)}, u32[]{:S(2)}) collective-permute-start(bf16[256,5120]{1,0:T(8,128)(2,1)} %collective-permute-done.2), channel_id=1, source_target_pairs={{0,4},{4,8},{8,12},{12,16},{16,20},{20,24},{24,28},{28,0},{1,5},{5... | collective-permute-start | bytes 7864328 | tf_op jit(solution)/shard_map/ppermute | solution.py:24
  457.2 264.1 %collective-permute-start.5 = (bf16[256,5120]{1,0:T(8,128)(2,1)}, bf16[256,5120]{1,0:T(8,128)(2,1)}, u32[]{:S(2)}, u32[]{:S(2)}) collective-permute-start(bf16[256,5120]{1,0:T(8,128)(2,1)} %collective-permute-done.3), channel_id=1, source_target_pairs={{0,28},{4,0},{8,4},{12,8},{16,12},{20,16},{24,20},{28,24},{1,29},{... | collective-permute-start | bytes 7864328 | tf_op jit(solution)/shard_map/ppermute | solution.py:27
  490.9 20.4 copy-start
  588.6 41.7 %copy-start.6 = (bf16[2048,1280]{0,1:T(8,128)(2,1)S(1)}, bf16[2048,1280]{0,1:T(8,128)(2,1)}, u32[]{:S(2)}) copy-start(bf16[2048,1280]{0,1:T(8,128)(2,1)} %all-gather.24.cloned.1.call-done) | copy-start | bytes 15728644
  588.6 41.7 %copy-start.8 = (bf16[2,256,2048]{2,1,0:T(8,128)(2,1)S(1)}, bf16[2,256,2048]{2,1,0:T(8,128)(2,1)}, u32[]{:S(2)}) copy-start(bf16[2,256,2048]{2,1,0:T(8,128)(2,1)} %param.14) | copy-start | bytes 6291460
  588.6 41.7 %copy-start.36 = (bf16[5,64,4,256]{3,1,2,0:T(8,128)(2,1)S(1)}, bf16[5,64,4,256]{3,1,2,0:T(8,128)(2,1)}, u32[]{:S(2)}) copy-start(bf16[5,64,4,256]{3,1,2,0:T(8,128)(2,1)} %convolution_convert_fusion.9) | copy-start | bytes 1966084
  593.3 1030.1 %copy-start.10 = (f32[256,2048]{1,0:T(8,128)}, f32[256,2048]{1,0:T(8,128)S(1)}, u32[]{:S(2)}) copy-start(f32[256,2048]{1,0:T(8,128)S(1)} %get-tuple-element.185) | copy-start | bytes 6291460
  627.6 97.2 %collective-permute-start.6 = (bf16[256,5120]{1,0:T(8,128)(2,1)}, bf16[256,5120]{1,0:T(8,128)(2,1)S(1)}, u32[]{:S(2)}, u32[]{:S(2)}) collective-permute-start(bf16[256,5120]{1,0:T(8,128)(2,1)} %collective-permute-done.4), channel_id=1, source_target_pairs={{0,4},{4,8},{8,12},{12,16},{16,20},{20,24},{24,28},{28,0},{1,5},{5... | collective-permute-start | bytes 7864328 | tf_op jit(solution)/shard_map/ppermute | solution.py:24
  633.4 875.9 %copy-start.40 = (bf16[256,2048]{1,0:T(8,128)(2,1)}, bf16[256,2048]{1,0:T(8,128)(2,1)S(1)}, u32[]{:S(2)}) copy-start(bf16[256,2048]{1,0:T(8,128)(2,1)S(1)} %multiply_convert_fusion.7) | copy-start | bytes 3145732
  1528.0 12.2 copy-start.49
  1554.0 24.8 copy-start.67
  1554.0 12.6 copy-start.43
  1597.5 12.2 copy-start.50
  1609.7 13.7 copy-start.92
  1609.7 13.7 copy-start.95
  1657.3 14.4 copy-start.27
  1676.8 87.7 %reduce-scatter.6.cloned.1.call-start = ((), (), s32[]{:S(2)}) async-start(), calls=%async_computation.22 | async-start | bytes 1638400 | tf_op jit(solution)/shard_map/reduce_scatter | solution.py:239
  1698.2 18.4 copy-start.25
  1730.5 217.6 %all-gather.38.cloned.1.call-start = ((), (), s32[]{:S(2)}) async-start(), calls=%async_computation.23 | async-start | bytes 10485760 | tf_op jit(solution)/shard_map/all_gather | solution.py:291
  1733.8 227.8 %all-gather.40.cloned.1.call-start = ((), (), s32[]{:S(2)}) async-start(), calls=%async_computation.24 | async-start | bytes 10485760 | tf_op jit(solution)/shard_map/all_gather | solution.py:292
  1735.3 313.8 %all-gather.42.cloned.1.call-start = ((), (), s32[]{:S(2)}) async-start(), calls=%async_computation.25 | async-start | bytes 10485760 | tf_op jit(solution)/shard_map/all_gather | solution.py:293
  1740.0 28.0 %all-to-all-start.3 = ((bf16[512,4,320]{0,2,1:T(8,128)(2,1)}), bf16[512,4,320]{0,2,1:T(8,128)(2,1)S(1)}, u32[]{:S(2)}, u32[]{:S(2)}) async-start(bf16[512,4,320]{0,2,1:T(8,128)(2,1)} %pad_maximum_fusion.12), calls=%async_computation.5 | async-start | bytes 2621440 | tf_op jit(solution)/shard_map/all_to_all | solution.py:285
  1768.0 31.8 %all-to-all-start = ((bf16[512,4,320]{0,2,1:T(8,128)(2,1)}), bf16[512,4,320]{0,2,1:T(8,128)(2,1)S(1)}, u32[]{:S(2)}, u32[]{:S(2)}) async-start(bf16[512,4,320]{0,2,1:T(8,128)(2,1)} %pad_maximum_fusion.11), calls=%async_computation.2 | async-start | bytes 2621440 | tf_op jit(solution)/shard_map/all_to_all | solution.py:282
  1799.8 14.7 all-to-all-start.2
  1814.6 14.0 all-to-all-start.1
  1829.3 106.1 %all-to-all-start.5 = ((bf16[512,4,1280]{2,0,1:T(8,128)(2,1)}), bf16[512,4,1280]{2,0,1:T(8,128)(2,1)}, u32[]{:S(2)}, u32[]{:S(2)}) async-start(bf16[512,4,1280]{2,0,1:T(8,128)(2,1)} %bitcast.382), calls=%async_computation.7 | async-start | bytes 10485760 | tf_op jit(solution)/shard_map/all_to_all | solution.py:287
  1834.4 317.0 %all-gather.44.cloned.1.call-start = ((), (), s32[]{:S(2)}) async-start(), calls=%async_computation.26 | async-start | bytes 10485760 | tf_op jit(solution)/shard_map/all_gather | solution.py:294
  1935.4 108.6 %all-to-all-start.4 = ((bf16[512,4,1280]{2,0,1:T(8,128)(2,1)}), bf16[512,4,1280]{2,0,1:T(8,128)(2,1)}, u32[]{:S(2)}, u32[]{:S(2)}) async-start(bf16[512,4,1280]{2,0,1:T(8,128)(2,1)} %bitcast.381), calls=%async_computation.6 | async-start | bytes 10485760 | tf_op jit(solution)/shard_map/all_to_all | solution.py:286
  2044.0 109.5 %all-to-all-start.6 = ((bf16[512,4,1280]{2,0,1:T(8,128)(2,1)}), bf16[512,4,1280]{2,0,1:T(8,128)(2,1)}, u32[]{:S(2)}, u32[]{:S(2)}) async-start(bf16[512,4,1280]{2,0,1:T(8,128)(2,1)} %bitcast.380), calls=%async_computation.8 | async-start | bytes 10485760 | tf_op jit(solution)/shard_map/all_to_all | solution.py:288
  2049.1 438.5 %reduce-scatter.8.cloned.1.call-start = ((), (), s32[]{:S(2)}) async-start(), calls=%async_computation.27 | async-start | bytes 21381120 | tf_op jit(solution)/shard_map/reduce_scatter | solution.py:301
  2049.2 16.9 copy-start.110
  2171.9 12.4 copy-start.93
  2171.9 27.8 %slice-start = ((s8[5242880]{0:T(1024)(128)(4,1)}), s8[4194304]{0:T(1024)(128)(4,1)S(1)}, s32[]{:S(2)}) async-start(s8[5242880]{0:T(1024)(128)(4,1)} %bitcast.378), calls=%async_computation.28 | async-start | bytes 8388608
  2184.4 12.5 copy-start.68
  2184.4 15.4 slice-start.1
  (81 other events, 270.7 us)
Sparse Core Ops, SparseCore 0:
  16.0 42.6 all-gather.15
  60.8 40.9 all-gather.17
  103.3 30.2 all-gather.25
  135.0 23.7 all-gather.31
  160.2 25.5 all-gather.29
  187.8 18.3 all-gather.19
  208.3 18.3 all-gather.35
  228.7 186.9 all-gather.21
  417.7 170.8 all-gather.23
  589.9 499.4 all-gather.27
  1090.9 406.6 all-gather.33
  1676.9 26.4 reduce-scatter.3
  1730.6 33.8 reduce-scatter.5
  1766.5 79.0 all-gather.37
  1847.0 97.3 all-gather.39
  1945.8 101.1 all-gather.41
  2048.4 102.9 all-gather.43
  2170.5 317.1 reduce-scatter.7
